TPU v7x, 32 devices: a whole 2x2x4 slice. The times are simulated.
32 devices in a mesh: grp: 8 (over z, core), tp: 4 (over y, x).
Axes of the slice: x: 2, y: 2, z: 4, core: 2. Of those that a mesh axis runs over, the one named last changes fastest.
Arguments:
- hidden: bfloat16 [128, 16384], P(('grp', 'tp')), may hold values from -130 to 130
- gain: float32 [16384], replicated, may hold values from 0.5 to 1.5
- head: bfloat16 [16384, 16384], P(None, ('grp', 'tp')), may hold values from -3 to 3
Outputs:
- log_probs: float32 [128, 16384], P(('grp', 'tp'))
All inputs are finite; a program needn't handle non-finite values.
Results may differ from a plain program's by a relative error of at most 0.00055.
Values may be sent and summed in bfloat16 or wider, within the bound.
No kernel may reach another device: no remote copies, remote signals or barrier semaphores. Data moves between devices by JAX's collectives and lax.ppermute only.
A program may use at most 128 MiB of HBM per device.

v0:
```python
import jax
import jax.numpy as jnp
from jax import lax
from jax.sharding import PartitionSpec as P


def on_device(hidden, gain, head):
    values = hidden.astype(jnp.float32)
    mean_square = jnp.mean(values * values, axis=-1, keepdims=True)
    normed = (values * lax.rsqrt(mean_square + 1e-05) * gain).astype(jnp.bfloat16)
    group_block = lax.all_gather(normed, "tp", axis=0, tiled=True)
    logits = jnp.dot(
        lax.all_gather(group_block, "grp", axis=0, tiled=True),
        head,
        preferred_element_type=jnp.float32,
    )
    owned = lax.all_to_all(logits, ("grp", "tp"), split_axis=0, concat_axis=1, tiled=True)
    top = jnp.max(owned, axis=-1, keepdims=True)
    total = jnp.sum(jnp.exp(owned - top), axis=-1, keepdims=True)
    return owned - top - jnp.log(total)


def solution(mesh):
    return jax.shard_map(
        on_device,
        mesh=mesh,
        in_specs=(P(("grp", "tp"), None), P(), P(None, ("grp", "tp"))),
        out_specs=P(("grp", "tp"), None),
        check_vma=False,
    )
```

profile of v0, /device:TPU:0, one launch (start us, length us, event | category | flops | bytes accessed | tf_op | source)
XLA Modules:
  0.0 100.4 jit_solution(16595028020233734949)
XLA Ops:
  6.5 0.0 all-gather.3.cloned.1.call-start
  6.5 1.2 %fusion = f32[4]{0:T(128)S(1)} fusion(bf16[4,16384]{1,0:T(4,128)(2,1)} %param.3), kind=kLoop, calls=%fused_computation.2 | loop fusion | flops 196604 | bytes 131088 | tf_op jit(solution)/shard_map/reduce_sum | solution.py:9
  7.7 1.0 %fusion.5 = bf16[1,4,16384]{2,1,0:T(4,128)(2,1)S(1)} fusion(bf16[4,16384]{1,0:T(4,128)(2,1)} %param.3, f32[16384]{0:T(1024)} %param.4, f32[4]{0:T(128)S(1)} %add_rsqrt_fusion), kind=kLoop, calls=%fused_computation.9 | loop fusion | flops 262144 | bytes 327696
  8.7 11.5 %all-gather = bf16[4,4,16384]{2,1,0:T(4,128)(2,1)S(1)} all-gather(bf16[1,4,16384]{2,1,0:T(4,128)(2,1)S(1)} %fusion.5), channel_id=1, replica_groups=mesh['grp'=8,'tp'=4] {'tp'}, dimensions={0}, use_global_device_ids=true | all-gather | bytes 655360 | tf_op jit(solution)/shard_map/all_gather | solution.py:11
  20.3 0.9 reshape.22
  21.2 0.0 all-gather.3.cloned.1.call-update
  21.2 47.3 %all-gather.3.cloned.1.call-done = bf16[128,16384]{1,0:T(8,128)(2,1)} async-done(((bf16[16,16384]{1,0:T(8,128)(2,1)}), bf16[128,16384]{1,0:T(8,128)(2,1)}) %all-gather.3.cloned.1.call-update) | async-done | bytes 4194320 | tf_op jit(solution)/shard_map/all_gather | solution.py:13
  68.5 9.4 %fusion.6 = f32[128,512]{1,0:T(8,128)S(1)} fusion(bf16[128,16384]{1,0:T(8,128)(2,1)} %all-gather.3.cloned.1.call-done, bf16[16384,512]{1,0:T(8,128)(2,1)} %param.5), kind=kOutput, calls=%fused_computation.11 | convolution fusion | flops 2147483648 | bytes 21233664 | tf_op jit(solution)/shard_map/dot_general | solution.py:12
  77.9 0.1 all_to_all.14
  78.0 14.1 %all_to_all.19 = f32[32,4,512]{2,1,0:T(4,128)S(1)} all-to-all(f32[32,4,512]{2,1,0:T(4,128)S(1)} %all_to_all.14), channel_id=1, replica_groups=mesh['grp'=8,'tp'=4] {'grp','tp'}, dimensions={0} | all-to-all | bytes 524288 | tf_op jit(solution)/shard_map/all_to_all | solution.py:17
  92.1 0.3 reduce_max.9
  92.4 0.3 fusion.4
  92.7 0.8 subtract_subtract_fusion
  (2 shorter events, 0.0 us)
Async XLA Ops:
  6.5 62.0 %all-gather.3.cloned.1.call-start = ((), (), s32[]{:S(2)}) async-start(), calls=%async_computation.1 | async-start | bytes 4718592 | tf_op jit(solution)/shard_map/all_gather | solution.py:13
Sparse Core Ops, SparseCore 0:
  21.3 47.1 all-gather.2
where the time goes:
time: 101 us; the launch traced here: 100 us
  waiting for transfers between devices  47.3 us (47%)
  blocking collectives  25.7 us (25%)
  between operations  13.4 us (13%)
  matrix products  9.38 us (9%)
  other arithmetic  3.61 us (4%)
    all_gather x1, waiting for transfers between devices, on_device(): lax.all_gather(group_block, 'grp', axis=0, tiled=True)  47.3 us
    all_to_all x1, blocking collectives, on_device(): lax.all_to_all(logits, ('grp', 'tp'), split_axis=0, concat_axis=1, tiled=...  14.1 us
    all_gather x1, blocking collectives, on_device(): group_block = lax.all_gather(normed, 'tp', axis=0, tiled=True)  11.5 us
    dot_general x1, matrix products, on_device(): jnp.dot(lax.all_gather(group_block, 'grp', axis=0, tiled=True), head, pre...  9.38 us
  transfers between devices with their start and end apart: 1, of which 1 were waited for; matrix products, arithmetic and copies ran while one was open for 0% of the time, Pallas kernels for 0%

commit v1 on v0

--- a/solution.py
+++ b/solution.py
@@ -14,7 +14,12 @@
         head,
         preferred_element_type=jnp.float32,
     )
-    owned = lax.all_to_all(logits, ("grp", "tp"), split_axis=0, concat_axis=1, tiled=True)
+    owned = jnp.concatenate(
+        lax.all_to_all(
+            jnp.stack(jnp.split(logits, lax.axis_size(("grp", "tp")), axis=0)), ("grp", "tp"), 0, 0
+        ),
+        axis=1,
+    )
     top = jnp.max(owned, axis=-1, keepdims=True)
     total = jnp.sum(jnp.exp(owned - top), axis=-1, keepdims=True)
     return owned - top - jnp.log(total)

time: 101 us -> 101 us (level)
  no operation moved by 1% of the time
where the time goes in v1:
time: 101 us
  waiting for transfers between devices  47.3 us (47%)
  blocking collectives  25.7 us (25%)
  between operations  13.5 us (13%)
  matrix products  9.38 us (9%)
  other arithmetic  3.61 us (4%)
  local copies, waits for them, and re-layouts  1.25 us (1%)
    all_gather x1, waiting for transfers between devices, on_device(): lax.all_gather(group_block, 'grp', axis=0, tiled=True)  47.3 us
    all_to_all x1, blocking collectives, on_device(): lax.all_to_all(jnp.stack(jnp.split(logits, lax.axis_size(('grp', 'tp')),...  14.1 us
    all_gather x1, blocking collectives, on_device(): group_block = lax.all_gather(normed, 'tp', axis=0, tiled=True)  11.5 us
    dot_general x1, matrix products, on_device(): jnp.dot(lax.all_gather(group_block, 'grp', axis=0, tiled=True), head, pre...  9.38 us
  transfers between devices with their start and end apart: 1, of which 1 were waited for; matrix products, arithmetic and copies ran while one was open for 0% of the time, Pallas kernels for 0%

profile of v1, /device:TPU:0, one launch (start us, length us, event | category | flops | bytes accessed | tf_op | source)
XLA Modules:
  0.0 100.8 jit_solution(1186990782019695218)
XLA Ops:
  6.5 0.0 all-gather.3.cloned.1.call-start
  6.5 1.2 %fusion = f32[4]{0:T(128)S(1)} fusion(bf16[4,16384]{1,0:T(4,128)(2,1)} %param.3), kind=kLoop, calls=%fused_computation.2 | loop fusion | flops 196604 | bytes 131088 | tf_op jit(solution)/shard_map/reduce_sum | solution.py:9
  7.7 1.0 %fusion.5 = bf16[1,4,16384]{2,1,0:T(4,128)(2,1)S(1)} fusion(bf16[4,16384]{1,0:T(4,128)(2,1)} %param.3, f32[16384]{0:T(1024)} %param.4, f32[4]{0:T(128)S(1)} %add_rsqrt_fusion), kind=kLoop, calls=%fused_computation.9 | loop fusion | flops 262144 | bytes 327696
  8.7 11.5 %all-gather = bf16[4,4,16384]{2,1,0:T(4,128)(2,1)S(1)} all-gather(bf16[1,4,16384]{2,1,0:T(4,128)(2,1)S(1)} %fusion.5), channel_id=1, replica_groups=mesh['grp'=8,'tp'=4] {'tp'}, dimensions={0}, use_global_device_ids=true | all-gather | bytes 655360 | tf_op jit(solution)/shard_map/all_gather | solution.py:11
  20.3 0.9 reshape.27
  21.2 0.0 all-gather.3.cloned.1.call-update
  21.2 47.3 %all-gather.3.cloned.1.call-done = bf16[128,16384]{1,0:T(8,128)(2,1)} async-done(((bf16[16,16384]{1,0:T(8,128)(2,1)}), bf16[128,16384]{1,0:T(8,128)(2,1)}) %all-gather.3.cloned.1.call-update) | async-done | bytes 4194320 | tf_op jit(solution)/shard_map/all_gather | solution.py:13
  68.5 9.4 %fusion.6 = f32[128,512]{1,0:T(8,128)S(1)} fusion(bf16[128,16384]{1,0:T(8,128)(2,1)} %all-gather.3.cloned.1.call-done, bf16[16384,512]{1,0:T(8,128)(2,1)} %param.5), kind=kOutput, calls=%fused_computation.75 | convolution fusion | flops 2147483648 | bytes 21233664 | tf_op jit(solution)/shard_map/dot_general | solution.py:12
  78.4 14.1 %all_to_all.5 = f32[32,4,512]{2,1,0:T(4,128)S(1)} all-to-all(f32[32,4,512]{2,1,0:T(4,128)S(1)} %constant_dynamic-update-slice_fusion), channel_id=1, replica_groups=mesh['grp'=8,'tp'=4] {'grp','tp'}, dimensions={0} | all-to-all | bytes 524288 | tf_op jit(solution)/shard_map/all_to_all | solution.py:18
  92.5 0.3 reduce_max.9
  92.7 0.3 fusion.4
  93.1 0.8 subtract_subtract_fusion
  (34 shorter events, 0.3 us)
Async XLA Ops:
  6.5 62.0 %all-gather.3.cloned.1.call-start = ((), (), s32[]{:S(2)}) async-start(), calls=%async_computation.1 | async-start | bytes 4718592 | tf_op jit(solution)/shard_map/all_gather | solution.py:13
Sparse Core Ops, SparseCore 0:
  21.3 47.1 all-gather.2

commit v2 on v0

--- a/solution.py
+++ b/solution.py
@@ -8,7 +8,12 @@
     values = hidden.astype(jnp.float32)
     mean_square = jnp.mean(values * values, axis=-1, keepdims=True)
     normed = (values * lax.rsqrt(mean_square + 1e-05) * gain).astype(jnp.bfloat16)
-    group_block = lax.all_gather(normed, "tp", axis=0, tiled=True)
+    ring = [normed]
+    for hop in range(3):
+        ring.append(lax.ppermute(ring[-1], "tp", [(dev, (dev + 1) % 4) for dev in range(4)]))
+    group_block = jnp.roll(
+        jnp.concatenate(ring[::-1], axis=0), (lax.axis_index("tp") + 1) * ring[0].shape[0], axis=0
+    )
     logits = jnp.dot(
         lax.all_gather(group_block, "grp", axis=0, tiled=True),
         head,

time: 101 us -> 109 us (1.079)
  waiting for transfers between devices: 47.3 us -> 62.9 us
  blocking collectives: 25.7 us -> 14.1 us
  starting transfers between devices: 0.01 us -> 3.81 us
    ppermute x0 -> x3, waiting for transfers between devices: none -> 15.4 us  [on_device(): lax.ppermute(ring[-1], 'tp', [(dev, (dev + 1) % 4) for dev in range(4)])]
    all_gather x1 -> x0, blocking collectives: 11.5 us -> none  [on_device(): group_block = lax.all_gather(normed, 'tp', axis=0, tiled=True)]
    ppermute x0 -> x3, starting transfers between devices: none -> 3.81 us  [on_device(): lax.ppermute(ring[-1], 'tp', [(dev, (dev + 1) % 4) for dev in range(4)])]
  transfers between devices with their start and end apart: 1 -> 4, of which waited for: 1 -> 4; matrix products, arithmetic and copies ran while one was open for 0% -> 0% of each run, Pallas kernels for 0% -> 0%
where the time goes in v2:
time: 109 us
  waiting for transfers between devices  62.9 us (58%)
  blocking collectives  14.1 us (13%)
  between operations  13.4 us (12%)
  matrix products  9.38 us (9%)
  starting transfers between devices  3.81 us (3%)
  other arithmetic  3.61 us (3%)
  local copies, waits for them, and re-layouts  1.91 us (2%)
    all_gather x1, waiting for transfers between devices, on_device(): lax.all_gather(group_block, 'grp', axis=0, tiled=True)  47.5 us
    ppermute x3, waiting for transfers between devices, on_device(): lax.ppermute(ring[-1], 'tp', [(dev, (dev + 1) % 4) for dev in range(4)])  15.4 us
    all_to_all x1, blocking collectives, on_device(): lax.all_to_all(logits, ('grp', 'tp'), split_axis=0, concat_axis=1, tiled=...  14.1 us
    dot_general x1, matrix products, on_device(): jnp.dot(lax.all_gather(group_block, 'grp', axis=0, tiled=True), head, pre...  9.38 us
    ppermute x3, starting transfers between devices, on_device(): lax.ppermute(ring[-1], 'tp', [(dev, (dev + 1) % 4) for dev in range(4)])  3.81 us
  transfers between devices with their start and end apart: 4, of which 4 were waited for; matrix products, arithmetic and copies ran while one was open for 0% of the time, Pallas kernels for 0%

profile of v2, /device:TPU:0, one launch (start us, length us, event | category | flops | bytes accessed | tf_op | source)
XLA Modules:
  0.0 109.2 jit_solution(11134192929308538358)
XLA Ops:
  6.5 0.0 all-gather.2.cloned.1.call-start
  6.5 1.2 %fusion = f32[4]{0:T(128)S(1)} fusion(bf16[4,16384]{1,0:T(4,128)(2,1)} %param.3), kind=kLoop, calls=%fused_computation.2 | loop fusion | flops 196604 | bytes 131088 | tf_op jit(solution)/shard_map/reduce_sum | solution.py:9
  7.7 1.0 fusion.2
  8.7 3.0 %collective-permute-start = (bf16[4,16384]{1,0:T(4,128)(2,1)S(1)}, bf16[4,16384]{1,0:T(4,128)(2,1)S(1)}, u32[]{:S(2)}, u32[]{:S(2)}) collective-permute-start(bf16[4,16384]{1,0:T(4,128)(2,1)S(1)} %fusion.2), channel_id=1, source_target_pairs={{0,1},{1,2},{2,3},{3,0},{4,5},{5,6},{6,7},{7,4},{8,9},{9,10},{10,1... | collective-permute-start | bytes 393224 | tf_op jit(solution)/shard_map/ppermute | solution.py:13
  11.8 4.5 %collective-permute-done = bf16[4,16384]{1,0:T(4,128)(2,1)S(1)} collective-permute-done((bf16[4,16384]{1,0:T(4,128)(2,1)S(1)}, bf16[4,16384]{1,0:T(4,128)(2,1)S(1)}, u32[]{:S(2)}, u32[]{:S(2)}) %collective-permute-start) | collective-permute-done | bytes 131104 | tf_op jit(solution)/shard_map/ppermute | solution.py:13
  16.2 0.8 collective-permute-start.1
  17.0 5.1 %collective-permute-done.1 = bf16[4,16384]{1,0:T(4,128)(2,1)S(1)} collective-permute-done((bf16[4,16384]{1,0:T(4,128)(2,1)S(1)}, bf16[4,16384]{1,0:T(4,128)(2,1)S(1)}, u32[]{:S(2)}, u32[]{:S(2)}) %collective-permute-start.1) | collective-permute-done | bytes 131104 | tf_op jit(solution)/shard_map/ppermute | solution.py:13
  22.1 0.0 collective-permute-start.2
  22.1 5.9 %collective-permute-done.2 = bf16[4,16384]{1,0:T(4,128)(2,1)S(1)} collective-permute-done((bf16[4,16384]{1,0:T(4,128)(2,1)S(1)}, bf16[4,16384]{1,0:T(4,128)(2,1)S(1)}, u32[]{:S(2)}, u32[]{:S(2)}) %collective-permute-start.2) | collective-permute-done | bytes 131104 | tf_op jit(solution)/shard_map/ppermute | solution.py:13
  28.0 0.9 concatenate.6
  28.8 0.9 constant_dynamic-slice_fusion
  29.8 0.0 all-gather.2.cloned.1.call-update
  29.8 47.5 %all-gather.2.cloned.1.call-done = bf16[128,16384]{1,0:T(8,128)(2,1)} async-done(((bf16[16,16384]{1,0:T(8,128)(2,1)}), bf16[128,16384]{1,0:T(8,128)(2,1)}) %all-gather.2.cloned.1.call-update) | async-done | bytes 4194320 | tf_op jit(solution)/shard_map/all_gather | solution.py:18
  77.3 9.4 %fusion.5 = f32[128,512]{1,0:T(8,128)S(1)} fusion(bf16[128,16384]{1,0:T(8,128)(2,1)} %all-gather.2.cloned.1.call-done, bf16[16384,512]{1,0:T(8,128)(2,1)} %param.5), kind=kOutput, calls=%fused_computation.11 | convolution fusion | flops 2147483648 | bytes 21233664 | tf_op jit(solution)/shard_map/dot_general | solution.py:17
  86.7 0.1 all_to_all.14
  86.8 14.1 %all_to_all.19 = f32[32,4,512]{2,1,0:T(4,128)S(1)} all-to-all(f32[32,4,512]{2,1,0:T(4,128)S(1)} %all_to_all.14), channel_id=1, replica_groups=mesh['grp'=8,'tp'=4] {'grp','tp'}, dimensions={0} | all-to-all | bytes 524288 | tf_op jit(solution)/shard_map/all_to_all | solution.py:22
  101.0 0.3 reduce_max.9
  101.2 0.3 fusion.4
  101.5 0.8 subtract_subtract_fusion
  (2 shorter events, 0.0 us)
Async XLA Ops:
  6.5 70.8 %all-gather.2.cloned.1.call-start = ((), (), s32[]{:S(2)}) async-start(), calls=%async_computation.1 | async-start | bytes 4718592 | tf_op jit(solution)/shard_map/all_gather | solution.py:18
  8.7 7.5 %collective-permute-start = (bf16[4,16384]{1,0:T(4,128)(2,1)S(1)}, bf16[4,16384]{1,0:T(4,128)(2,1)S(1)}, u32[]{:S(2)}, u32[]{:S(2)}) collective-permute-start(bf16[4,16384]{1,0:T(4,128)(2,1)S(1)} %fusion.2), channel_id=1, source_target_pairs={{0,1},{1,2},{2,3},{3,0},{4,5},{5,6},{6,7},{7,4},{8,9},{9,10},{10,1... | collective-permute-start | bytes 393224 | tf_op jit(solution)/shard_map/ppermute | solution.py:13
  16.2 5.9 %collective-permute-start.1 = (bf16[4,16384]{1,0:T(4,128)(2,1)S(1)}, bf16[4,16384]{1,0:T(4,128)(2,1)S(1)}, u32[]{:S(2)}, u32[]{:S(2)}) collective-permute-start(bf16[4,16384]{1,0:T(4,128)(2,1)S(1)} %collective-permute-done), channel_id=1, source_target_pairs={{0,1},{1,2},{2,3},{3,0},{4,5},{5,6},{6,7},{7,4},{8,9},{9,10},{10,1... | collective-permute-start | bytes 393224 | tf_op jit(solution)/shard_map/ppermute | solution.py:13
  22.1 5.9 %collective-permute-start.2 = (bf16[4,16384]{1,0:T(4,128)(2,1)S(1)}, bf16[4,16384]{1,0:T(4,128)(2,1)S(1)}, u32[]{:S(2)}, u32[]{:S(2)}) collective-permute-start(bf16[4,16384]{1,0:T(4,128)(2,1)S(1)} %collective-permute-done.1), channel_id=1, source_target_pairs={{0,1},{1,2},{2,3},{3,0},{4,5},{5,6},{6,7},{7,4},{8,9},{9,10},{10,1... | collective-permute-start | bytes 393224 | tf_op jit(solution)/shard_map/ppermute | solution.py:13
Sparse Core Ops, SparseCore 0:
  29.9 47.3 all-gather.1
